TPU v7x, 256 devices: a whole 4x4x8 slice. The times are simulated.
256 devices in a mesh: depth: 64 (over x, z, core), strip: 4 (over y).
Axes of the slice: x: 4, y: 4, z: 8, core: 2. Of those that a mesh axis runs over, the one named last changes fastest.
Arguments:
- density: bfloat16 [256, 64, 1024], P('depth', 'strip'), may hold values from -6 to 6
- tf_bins: int32 [256, 64, 1024], P('depth', 'strip'), may hold values from 0 to 15
- tf_table: float32 [4, 16], replicated, may hold values from 0.2 to 2
- brick_order: int32 [4, 64], P('strip'), may hold values from 0 to 63, each once within a row
Outputs:
- image: float32 [4, 65536], P(None, ('strip', 'depth'))
Inputs may be any that keep to these rules, and one draw needn't show every extreme that they name: `tf_bins`: each voxel's bin indexes a column of tf_table. `brick_order`: each row lists every brick once.
All inputs are finite; a program needn't handle non-finite values.
Results may differ from a plain program's by a relative error of at most 0.0017.
Values may be sent and summed in bfloat16 or wider, within the bound.
A program may use at most 64 MiB of HBM per device.

v0:
```python
import jax
import jax.numpy as jnp
from jax import lax
from jax.sharding import PartitionSpec as P

LIGHT_X = 0.36
LIGHT_Y = 0.48
LIGHT_Z = 0.8
SHADE_GAIN = 1.5


def with_halo(cells, sides, width):
    for axis, dim in sides:
        count = lax.axis_size(axis)
        ends = count - 1
        head = lax.slice_in_dim(cells, 0, width, axis=dim)
        tail = lax.slice_in_dim(cells, cells.shape[dim] - width, cells.shape[dim], axis=dim)
        cells = jnp.concatenate(
            [
                lax.ppermute(tail, axis, [(i, (i + 1) % count) for i in range(ends)]),
                cells,
                lax.ppermute(head, axis, [((i + 1) % count, i) for i in range(ends)]),
            ],
            axis=dim,
        )
    return cells


def shear_plane(values, plane_index):
    across = values.shape[-1]
    offset = 3 * plane_index // 8
    fraction = (3 * plane_index % 8).astype(jnp.float32) / 8.0
    columns = jnp.arange(across, dtype=jnp.int32)
    first = jnp.where(columns < across - offset, jnp.roll(values, -offset, axis=2), 0.0)
    second = jnp.where(columns < across - offset - 1, jnp.roll(first, -1, axis=2), 0.0)
    return (1.0 - fraction) * first + fraction * second


def plane_terms(window, tf_plane, tf_table, plane_index, total_planes):
    beneath = window[0]
    middle = window[1]
    overhead = window[2]
    centre = middle[1:-1]
    sideways = jnp.pad(centre, ((0, 0), (1, 1)))
    slope_across = 0.5 * (sideways[:, 2:] - sideways[:, :-2])
    slope_down = 0.5 * (middle[2:] - middle[:-2])
    slope_deep = 0.5 * (overhead[1:-1] - beneath[1:-1])
    lengths = jnp.sqrt(
        1.0 + slope_across * slope_across + slope_down * slope_down + slope_deep * slope_deep
    )
    shading = (LIGHT_X * slope_across + LIGHT_Y * slope_down + LIGHT_Z * slope_deep) / lengths
    classes = jnp.arange(tf_table.shape[1], dtype=jnp.int32)
    onehot = (tf_plane[None, :, :] == classes[:, None, None]).astype(jnp.float32)
    looked = jnp.einsum("cm,myx->cyx", tf_table, onehot, precision=lax.Precision.HIGHEST)
    extinction = looked[0] * (1.0 + centre * centre) / total_planes
    opacity = 1.0 - jnp.exp(-extinction)
    emitted = looked[1:] * (opacity * jnp.exp(SHADE_GAIN * shading))[None]
    return shear_plane(jnp.concatenate([extinction[None], emitted], axis=0), plane_index)


def order_mask(sequence):
    bricks = sequence.shape[0]
    slots = jnp.arange(bricks, dtype=jnp.int32)
    onehot = (sequence[:, None] == slots[None, :]).astype(jnp.int32)
    position = jnp.sum(onehot * slots[:, None], axis=0)
    return (position[None, :] < position[:, None]).astype(jnp.float32)


def per_device(density, tf_bins, tf_table, brick_order):
    planes = density.shape[0]
    height = density.shape[1]
    across = density.shape[2]
    bricks = lax.axis_size("depth")
    block = with_halo(density, (("depth", 0), ("strip", 1)), 1)
    first_plane = lax.axis_index("depth") * planes
    total_planes = planes * bricks
    colour = jnp.zeros((3, height, across), jnp.float32)
    depth_sum = jnp.zeros((height, across), jnp.float32)
    for plane_at in range(planes):
        window = block[plane_at : plane_at + 3].astype(jnp.float32)
        sheared = plane_terms(
            window, tf_bins[plane_at], tf_table, first_plane + plane_at, total_planes
        )
        colour = colour + jnp.exp(-depth_sum)[None] * sheared[1:]
        depth_sum = depth_sum + sheared[0]
    pixels = height * across
    before = order_mask(brick_order[0])
    flat_colour = colour.reshape(3, pixels)
    flat_depth = depth_sum.reshape(1, pixels)
    partial_value = jnp.concatenate([flat_colour, flat_depth], axis=0)[:, None, :]
    received = lax.all_to_all(
        partial_value.astype(jnp.bfloat16), "depth", split_axis=2, concat_axis=1, tiled=True
    ).astype(partial_value.dtype)
    depths = received[3]
    prefix = jnp.dot(before, depths, precision=lax.Precision.HIGHEST)
    weight = jnp.exp(-prefix)
    shown = jnp.sum(weight[None] * received[:3], axis=1)
    remaining = jnp.exp(-jnp.sum(depths, axis=0))
    return jnp.concatenate([shown, remaining[None]], axis=0)


def solution(mesh):
    in_specs = (P("depth", "strip", None), P("depth", "strip", None), P(), P("strip", None))
    out_specs = P(None, ("strip", "depth"))
    return jax.shard_map(
        per_device, mesh=mesh, in_specs=in_specs, out_specs=out_specs, check_vma=False
    )
```

profile of v0, /device:TPU:1, one launch (start us, length us, event | category | flops | bytes accessed | tf_op | source)
XLA Modules:
  0.0 676.8 jit_solution(5689342530783288285)
XLA Ops:
  0.0 0.0 copy-start
  0.0 0.8 fusion.84
  0.8 4.9 collective-permute-start
  5.7 1.9 collective-permute-start.1
  7.7 1.0 slice_bitcast_fusion.1
  8.7 0.0 copy-done
  8.7 0.4 fusion.1
  9.1 0.4 convolution_bitcast_fusion.1
  9.6 0.4 fusion.2
  10.0 0.4 convolution_bitcast_fusion
  10.5 0.0 collective-permute-done
  10.5 0.9 constant_dynamic-update-slice_fusion.1
  11.4 0.0 collective-permute-done.1
  11.5 3.2 collective-permute-start.2
  14.7 1.3 collective-permute-start.3
  16.1 0.2 copy.133
  16.3 0.2 copy.132
  16.6 0.0 collective-permute-done.2
  16.6 2.6 collective-permute-done.3
  19.2 0.1 pad_maximum_fusion
  19.4 0.1 slice_convert_fusion.1
  19.6 0.2 fusion.61
  19.8 0.1 slice_multiply_fusion.3
  19.9 0.1 copy.84
  19.9 0.7 fusion.21
  20.6 0.2 slice.353
  20.9 0.2 fusion.17
  21.1 0.1 slice.365
  21.3 0.2 fusion.43
  21.5 0.1 slice_multiply_fusion.1
  21.6 0.1 copy.96
  21.7 0.7 fusion.9
  22.3 0.2 slice.389
  22.6 0.2 broadcast_multiply_fusion
  22.8 0.1 slice.377
  22.9 0.2 fusion.29
  23.2 0.7 fusion.27
  23.8 0.1 slice.355
  23.9 0.2 negate_exponential_fusion.1
  24.2 0.1 pad_maximum_fusion.1
  24.2 0.3 copy_add_fusion
  24.6 0.7 fusion.31
  25.2 0.2 negate_exponential_fusion
  25.4 0.1 fusion.33
  25.6 0.3 fusion.24
  25.9 0.1 pad_maximum_fusion.2
  26.0 13.2 %copy.98 = bf16[4,1,16384]{0,1,2:T(2,128)(2,1)} copy(bf16[4,1,16384]{2,0,1:T(4,128)(2,1)S(1)} %pad_maximum_fusion.2) | data formatting | bytes 262144 | tf_op jit(solution)/shard_map/concatenate | solution.py:90
  39.2 0.5 broadcast.130
  39.7 0.0 copy-start.2
  39.7 90.8 %reduce.6 = bf16[16384,4]{1,0:T(8,128)(2,1)} reduce(bf16[16384,1,4]{2,1,0:T(2,128)(2,1)} %bitcast.201, bf16[]{:T(256)} %broadcast.130), dimensions={1}, to_apply=%bitcast.190.reduce_sub_computation | reduce | bytes 262146
  130.4 9.3 %reshape.196 = bf16[64,2,512]{2,1,0:T(2,128)(2,1)} reshape(bf16[16384,4]{1,0:T(8,128)(2,1)} %reduce.6) | data formatting | bytes 262144
  139.8 14.3 %all-to-all-start = ((bf16[64,2,512]{2,1,0:T(2,128)(2,1)}), bf16[64,2,512]{2,1,0:T(2,128)(2,1)S(1)}, u32[]{:S(2)}, u32[]{:S(2)}) async-start(bf16[64,2,512]{2,1,0:T(2,128)(2,1)} %reshape.196), calls=%async_computation | async-start | bytes 262144 | tf_op jit(solution)/shard_map/all_to_all | solution.py:91
  154.1 0.0 copy-done.2
  154.1 0.1 select_reduce_fusion
  154.2 10.2 %all-to-all-done = bf16[64,2,512]{2,1,0:T(2,128)(2,1)S(1)} async-done(((bf16[64,2,512]{2,1,0:T(2,128)(2,1)}), bf16[64,2,512]{2,1,0:T(2,128)(2,1)S(1)}, u32[]{:S(2)}, u32[]{:S(2)}) %all-to-all-start) | async-done | bytes 131104 | tf_op jit(solution)/shard_map/all_to_all | solution.py:91
  164.4 17.1 %reshape.197 = bf16[16384,1,4]{2,1,0:T(2,128)(2,1)} reshape(bf16[64,2,512]{2,1,0:T(2,128)(2,1)S(1)} %all-to-all-done) | data formatting | bytes 262144
  181.5 11.0 %slice.394 = f32[3,1,16384]{0,1,2:T(1,128)} slice(bf16[4,1,16384]{0,1,2:T(2,128)(2,1)} %bitcast.199), slice={[0:3], [0:1], [0:16384]} | slice | bytes 393216 | tf_op jit(solution)/shard_map/slice | solution.py:97
  192.6 0.0 copy-done.1
  192.6 233.5 %slice_reduce_fusion.1 = bf16[16384]{0:T(1024)(128)(2,1)S(1)} fusion(bf16[4,1,16384]{0,1,2:T(2,128)(2,1)S(1)} %bitcast.200), kind=kLoop, calls=%fused_computation.1 | loop fusion | bytes 65536 | tf_op jit(solution)/shard_map/slice | solution.py:94
  426.0 9.9 %bitcast_convert_fusion = f32[4,1,16384]{0,1,2:T(1,128)} fusion(bf16[16384,1,4]{2,1,0:T(2,128)(2,1)S(1)} %copy-done.1), kind=kLoop, calls=%fused_computation.204 | loop fusion | flops 65536 | bytes 393216 | tf_op jit(solution)/shard_map/convert_element_type | solution.py:93
  435.9 5.2 copy.100
  441.1 234.7 %slice_reduce_fusion = f32[16384]{0:T(1024)S(1)} fusion(f32[4,1,16384]{0,1,2:T(1,128)} %bitcast_convert_fusion), kind=kLoop, calls=%fused_computation | loop fusion | bytes 131072 | tf_op jit(solution)/shard_map/slice | solution.py:94
  675.9 0.2 fusion
  676.2 0.6 pad_maximum_fusion.3
  (33 shorter events, 0.5 us)
Async XLA Ops:
  0.0 8.7 %copy-start = (f32[4,16]{1,0:T(4,128)S(1)}, f32[4,16]{1,0:T(4,128)}, u32[]{:S(2)}) copy-start(f32[4,16]{1,0:T(4,128)} %param.8) | copy-start | bytes 772
  0.8 9.7 %collective-permute-start = (bf16[1,16,1024]{2,1,0:T(8,128)(2,1)S(1)}, bf16[1,16,1024]{2,1,0:T(8,128)(2,1)S(1)}, u32[]{:S(2)}, u32[]{:S(2)}) collective-permute-start(bf16[1,16,1024]{2,1,0:T(8,128)(2,1)S(1)} %get-tuple-element.32), channel_id=1, source_target_pairs={{0,4},{4,8},{8,12},{12,16},{16,20},{20,24},{24,28},{28,32},{32,36}... | collective-permute-start | bytes 98312 | tf_op jit(solution)/shard_map/ppermute | solution.py:20
  5.7 5.7 collective-permute-start.1
  11.5 5.2 collective-permute-start.2
  14.7 4.6 collective-permute-start.3
  39.7 114.4 %copy-start.2 = (s32[1,64]{1,0:T(1,128)S(1)}, s32[1,64]{1,0:T(1,128)}, u32[]{:S(2)}) copy-start(s32[1,64]{1,0:T(1,128)} %param.9) | copy-start | bytes 772
  139.8 24.7 %all-to-all-start = ((bf16[64,2,512]{2,1,0:T(2,128)(2,1)}), bf16[64,2,512]{2,1,0:T(2,128)(2,1)S(1)}, u32[]{:S(2)}, u32[]{:S(2)}) async-start(bf16[64,2,512]{2,1,0:T(2,128)(2,1)} %reshape.196), calls=%async_computation | async-start | bytes 262144 | tf_op jit(solution)/shard_map/all_to_all | solution.py:91
  181.5 11.0 %copy-start.1 = (bf16[16384,1,4]{2,1,0:T(2,128)(2,1)S(1)}, bf16[16384,1,4]{2,1,0:T(2,128)(2,1)}, u32[]{:S(2)}) copy-start(bf16[16384,1,4]{2,1,0:T(2,128)(2,1)} %reshape.197) | copy-start | bytes 393220
where the time goes:
time: 677 us
  local copies, waits for them, and re-layouts  529 us (78%)
  other arithmetic  107 us (16%)
  starting transfers between devices  25.7 us (4%)
  waiting for transfers between devices  12.8 us (2%)
    slice x3, local copies, waits for them, and re-layouts, per_device(): depths = received[3]  468 us
    unnamed x1, other arithmetic  90.8 us
    unnamed x14, local copies, waits for them, and re-layouts  27.9 us
    slice x2, local copies, waits for them, and re-layouts, per_device(): shown = jnp.sum(weight[None] * received[:3], axis=1)  16.2 us
    all_to_all x1, starting transfers between devices, per_device(): lax.all_to_all(partial_value.astype(jnp.bfloat16), 'depth', split_axis=2,...  14.3 us
  transfers between devices with their start and end apart: 5, of which 2 were waited for; matrix products, arithmetic and copies ran while one was open for 1% of the time, Pallas kernels for 0%

commit v1 on v0

--- a/solution.py
+++ b/solution.py
@@ -7,6 +7,13 @@
 LIGHT_Y = 0.48
 LIGHT_Z = 0.8
 SHADE_GAIN = 1.5
+
+
+def stacked_exchange(array, mesh_axis, split, join):
+    size = lax.axis_size(mesh_axis)
+    blocks = jnp.stack(jnp.split(array, size, axis=split), axis=0)
+    blocks = lax.all_to_all(blocks, mesh_axis, split_axis=0, concat_axis=0)
+    return jnp.concatenate(blocks, axis=join)
 
 
 def with_halo(cells, sides, width):
@@ -88,9 +95,9 @@
     flat_colour = colour.reshape(3, pixels)
     flat_depth = depth_sum.reshape(1, pixels)
     partial_value = jnp.concatenate([flat_colour, flat_depth], axis=0)[:, None, :]
-    received = lax.all_to_all(
-        partial_value.astype(jnp.bfloat16), "depth", split_axis=2, concat_axis=1, tiled=True
-    ).astype(partial_value.dtype)
+    received = stacked_exchange(partial_value.astype(jnp.bfloat16), "depth", 2, 1).astype(
+        partial_value.dtype
+    )
     depths = received[3]
     prefix = jnp.dot(before, depths, precision=lax.Precision.HIGHEST)
     weight = jnp.exp(-prefix)

time: 677 us -> 86.6 us (0.13)
  local copies, waits for them, and re-layouts: 529 us -> 3.39 us
  other arithmetic: 107 us -> 44.1 us
    slice x3 -> x1, local copies, waits for them, and re-layouts: 468 us -> 0.07 us  [per_device(): depths = received[3]]
    unnamed x1 -> x63, other arithmetic: 90.8 us -> 37.1 us
    unnamed x14 -> x13, local copies, waits for them, and re-layouts: 27.9 us -> 1.12 us
    slice x2 -> x0, local copies, waits for them, and re-layouts: 16.2 us -> none  [per_device(): shown = jnp.sum(weight[None] * received[:3], axis=1)]
    concatenate x1 -> x0, local copies, waits for them, and re-layouts: 13.2 us -> none  [per_device(): jnp.concatenate([flat_colour, flat_depth], axis=0)[:, None, :]]
    convert_element_type x1, other arithmetic: 9.87 us -> 0.02 us  [per_device(): stacked_exchange(partial_value.astype(jnp.bfloat16), 'depth', 2, 1)]
  transfers between devices with their start and end apart: 5 -> 5, of which waited for: 2 -> 3; matrix products, arithmetic and copies ran while one was open for 1% -> 3% of each run, Pallas kernels for 0% -> 0%
where the time goes in v1:
time: 86.6 us; the launch traced here: 86.1 us
  other arithmetic  44.1 us (51%)
  starting transfers between devices  25.2 us (29%)
  waiting for transfers between devices  10.8 us (12%)
  local copies, waits for them, and re-layouts  3.39 us (4%)
  matrix products  1.85 us (2%)
    unnamed x63, other arithmetic  37.1 us
    all_to_all x1, starting transfers between devices, stacked_exchange(): blocks = lax.all_to_all(blocks, mesh_axis, split_axis=0, concat_axis=0)  13.1 us
    all_to_all x1, waiting for transfers between devices, stacked_exchange(): blocks = lax.all_to_all(blocks, mesh_axis, split_axis=0, concat_axis=0)  9.58 us
    ppermute x2, starting transfers between devices, with_halo(): lax.ppermute(tail, axis, [(i, (i + 1) % count) for i in range(ends)])  8.9 us
    ppermute x2, starting transfers between devices, with_halo(): lax.ppermute(head, axis, [((i + 1) % count, i) for i in range(ends)])  3.21 us
    add x4, other arithmetic, shear_plane(): return (1.0 - fraction) * first + fraction * second  1.88 us
  transfers between devices with their start and end apart: 5, of which 3 were waited for; matrix products, arithmetic and copies ran while one was open for 3% of the time, Pallas kernels for 0%

profile of v1, /device:TPU:1, one launch (start us, length us, event | category | flops | bytes accessed | tf_op | source)
XLA Modules:
  0.0 86.1 jit_solution(4554565502898780992)
XLA Ops:
  0.0 0.8 fusion.152
  0.8 4.9 %collective-permute-start = (bf16[1,16,1024]{2,1,0:T(8,128)(2,1)S(1)}, bf16[1,16,1024]{2,1,0:T(8,128)(2,1)S(1)}, u32[]{:S(2)}, u32[]{:S(2)}) collective-permute-start(bf16[1,16,1024]{2,1,0:T(8,128)(2,1)S(1)} %get-tuple-element.32), channel_id=1, source_target_pairs={{0,4},{4,8},{8,12},{12,16},{16,20},{20,24},{24,28},{28,32},{32,36}... | collective-permute-start | bytes 98312 | tf_op jit(solution)/shard_map/ppermute | solution.py:27
  5.7 1.9 %collective-permute-start.1 = (bf16[1,16,1024]{2,1,0:T(8,128)(2,1)S(1)}, bf16[1,16,1024]{2,1,0:T(8,128)(2,1)S(1)}, u32[]{:S(2)}, u32[]{:S(2)}) collective-permute-start(bf16[1,16,1024]{2,1,0:T(8,128)(2,1)S(1)} %get-tuple-element.31), channel_id=1, source_target_pairs={{4,0},{8,4},{12,8},{16,12},{20,16},{24,20},{28,24},{32,28},{36,32}... | collective-permute-start | bytes 98312 | tf_op jit(solution)/shard_map/ppermute | solution.py:29
  10.0 1.0 %collective-permute-done.1 = bf16[1,16,1024]{2,1,0:T(8,128)(2,1)S(1)} collective-permute-done((bf16[1,16,1024]{2,1,0:T(8,128)(2,1)S(1)}, bf16[1,16,1024]{2,1,0:T(8,128)(2,1)S(1)}, u32[]{:S(2)}, u32[]{:S(2)}) %collective-permute-start.1) | collective-permute-done | bytes 32800 | tf_op jit(solution)/shard_map/ppermute | solution.py:29
  11.0 1.3 %collective-permute-start.3 = (bf16[6,1,1024]{2,1,0:T(2,128)(2,1)S(1)}, bf16[6,1,1024]{2,1,0:T(2,128)(2,1)S(1)}, u32[]{:S(2)}, u32[]{:S(2)}) collective-permute-start(bf16[6,1,1024]{2,1,0:T(2,128)(2,1)S(1)} %get-tuple-element.30), channel_id=1, source_target_pairs={{1,0},{2,1},{3,2},{5,4},{6,5},{7,6},{9,8},{10,9},{11,10},{13,12},{... | collective-permute-start | bytes 36872 | tf_op jit(solution)/shard_map/ppermute | solution.py:29
  12.3 4.0 %collective-permute-start.2 = (bf16[6,1,1024]{2,1,0:T(2,128)(2,1)S(1)}, bf16[6,1,1024]{2,1,0:T(2,128)(2,1)S(1)}, u32[]{:S(2)}, u32[]{:S(2)}) collective-permute-start(bf16[6,1,1024]{2,1,0:T(2,128)(2,1)S(1)} %get-tuple-element.29), channel_id=1, source_target_pairs={{0,1},{1,2},{2,3},{4,5},{5,6},{6,7},{8,9},{9,10},{10,11},{12,13},{... | collective-permute-start | bytes 36872 | tf_op jit(solution)/shard_map/ppermute | solution.py:27
  18.3 0.7 fusion.21
  20.1 0.7 fusion.9
  21.2 0.7 fusion.29
  22.6 0.7 fusion.33
  23.9 0.6 constant_dynamic-update-slice_fusion.66
  24.4 0.6 constant_dynamic-update-slice_fusion.65
  25.6 0.6 constant_dynamic-update-slice_fusion.63
  26.2 0.6 constant_dynamic-update-slice_fusion.62
  26.8 0.6 constant_dynamic-update-slice_fusion.61
  27.4 0.6 constant_dynamic-update-slice_fusion.60
  29.1 0.6 constant_dynamic-update-slice_fusion.57
  30.3 0.6 constant_dynamic-update-slice_fusion.55
  30.9 0.6 constant_dynamic-update-slice_fusion.54
  31.5 0.6 constant_dynamic-update-slice_fusion.53
  32.1 0.6 constant_dynamic-update-slice_fusion.52
  32.7 0.6 constant_dynamic-update-slice_fusion.51
  33.3 0.6 constant_dynamic-update-slice_fusion.50
  33.8 0.6 constant_dynamic-update-slice_fusion.49
  34.5 0.6 constant_dynamic-update-slice_fusion.48
  35.0 0.6 constant_dynamic-update-slice_fusion.47
  35.6 0.6 constant_dynamic-update-slice_fusion.46
  36.8 0.6 constant_dynamic-update-slice_fusion.44
  37.4 0.6 constant_dynamic-update-slice_fusion.43
  38.0 0.6 constant_dynamic-update-slice_fusion.42
  38.6 0.6 constant_dynamic-update-slice_fusion.41
  39.2 0.6 constant_dynamic-update-slice_fusion.40
  39.8 0.6 constant_dynamic-update-slice_fusion.39
  40.9 0.6 constant_dynamic-update-slice_fusion.37
  42.1 0.6 constant_dynamic-update-slice_fusion.35
  42.7 0.6 constant_dynamic-update-slice_fusion.34
  43.9 0.6 constant_dynamic-update-slice_fusion.32
  45.0 0.6 constant_dynamic-update-slice_fusion.30
  45.6 0.6 constant_dynamic-update-slice_fusion.29
  46.2 0.6 constant_dynamic-update-slice_fusion.28
  46.8 0.6 constant_dynamic-update-slice_fusion.27
  47.4 0.6 constant_dynamic-update-slice_fusion.26
  48.0 0.6 constant_dynamic-update-slice_fusion.25
  48.6 0.6 constant_dynamic-update-slice_fusion.24
  49.8 0.6 constant_dynamic-update-slice_fusion.22
  50.4 0.6 constant_dynamic-update-slice_fusion.21
  51.0 0.6 constant_dynamic-update-slice_fusion.20
  51.5 0.6 constant_dynamic-update-slice_fusion.19
  52.1 0.6 constant_dynamic-update-slice_fusion.18
  52.7 0.6 constant_dynamic-update-slice_fusion.17
  53.3 0.6 constant_dynamic-update-slice_fusion.16
  53.9 0.6 constant_dynamic-update-slice_fusion.15
  55.1 0.6 constant_dynamic-update-slice_fusion.13
  56.3 0.6 constant_dynamic-update-slice_fusion.11
  57.4 0.6 constant_dynamic-update-slice_fusion.9
  58.6 0.6 constant_dynamic-update-slice_fusion.7
  59.2 0.6 constant_dynamic-update-slice_fusion.6
  59.8 0.6 constant_dynamic-update-slice_fusion.5
  60.4 0.6 constant_dynamic-update-slice_fusion.4
  61.0 0.6 constant_dynamic-update-slice_fusion.3
  61.6 13.1 %all-to-all-start = ((bf16[64,4,1,256]{3,1,2,0:T(4,128)(2,1)}), bf16[64,4,1,256]{3,1,2,0:T(4,128)(2,1)S(1)}, u32[]{:S(2)}, u32[]{:S(2)}) async-start(bf16[64,4,1,256]{3,1,2,0:T(4,128)(2,1)} %constant_dynamic-update-slice_fusion.3), calls=%async_computation | async-start | bytes 262144 | tf_op jit(solution)/shard_map/all_to_all | solution.py:15
  74.7 0.6 copy-done.3
  75.4 9.6 %all-to-all-done = bf16[64,4,1,256]{3,1,2,0:T(4,128)(2,1)S(1)} async-done(((bf16[64,4,1,256]{3,1,2,0:T(4,128)(2,1)}), bf16[64,4,1,256]{3,1,2,0:T(4,128)(2,1)S(1)}, u32[]{:S(2)}, u32[]{:S(2)}) %all-to-all-start) | async-done | bytes 131104 | tf_op jit(solution)/shard_map/all_to_all | solution.py:15
  85.5 0.6 pad_maximum_fusion.2
  (88 shorter events, 15.3 us)
Async XLA Ops:
  0.0 7.8 %copy-start = (f32[4,16]{1,0:T(4,128)S(1)}, f32[4,16]{1,0:T(4,128)}, u32[]{:S(2)}) copy-start(f32[4,16]{1,0:T(4,128)} %param.8) | copy-start | bytes 772
  0.0 7.7 %copy-start.2 = (s32[4,16,1024]{2,1,0:T(8,128)S(1)}, s32[4,16,1024]{2,1,0:T(8,128)}, u32[]{:S(2)}) copy-start(s32[4,16,1024]{2,1,0:T(8,128)} %param.7) | copy-start | bytes 786436
  0.8 8.7 %collective-permute-start = (bf16[1,16,1024]{2,1,0:T(8,128)(2,1)S(1)}, bf16[1,16,1024]{2,1,0:T(8,128)(2,1)S(1)}, u32[]{:S(2)}, u32[]{:S(2)}) collective-permute-start(bf16[1,16,1024]{2,1,0:T(8,128)(2,1)S(1)} %get-tuple-element.32), channel_id=1, source_target_pairs={{0,4},{4,8},{8,12},{12,16},{16,20},{20,24},{24,28},{28,32},{32,36}... | collective-permute-start | bytes 98312 | tf_op jit(solution)/shard_map/ppermute | solution.py:27
  5.7 5.2 %collective-permute-start.1 = (bf16[1,16,1024]{2,1,0:T(8,128)(2,1)S(1)}, bf16[1,16,1024]{2,1,0:T(8,128)(2,1)S(1)}, u32[]{:S(2)}, u32[]{:S(2)}) collective-permute-start(bf16[1,16,1024]{2,1,0:T(8,128)(2,1)S(1)} %get-tuple-element.31), channel_id=1, source_target_pairs={{4,0},{8,4},{12,8},{16,12},{20,16},{24,20},{28,24},{32,28},{36,32}... | collective-permute-start | bytes 98312 | tf_op jit(solution)/shard_map/ppermute | solution.py:29
  9.1 0.9 %copy-start.1 = (bf16[4,16,1024]{2,1,0:T(8,128)(2,1)S(1)}, bf16[4,16,1024]{2,1,0:T(8,128)(2,1)}, u32[]{:S(2)}) copy-start(bf16[4,16,1024]{2,1,0:T(8,128)(2,1)} %param.6) | copy-start | bytes 393220
  11.0 5.9 %collective-permute-start.3 = (bf16[6,1,1024]{2,1,0:T(2,128)(2,1)S(1)}, bf16[6,1,1024]{2,1,0:T(2,128)(2,1)S(1)}, u32[]{:S(2)}, u32[]{:S(2)}) collective-permute-start(bf16[6,1,1024]{2,1,0:T(2,128)(2,1)S(1)} %get-tuple-element.30), channel_id=1, source_target_pairs={{1,0},{2,1},{3,2},{5,4},{6,5},{7,6},{9,8},{10,9},{11,10},{13,12},{... | collective-permute-start | bytes 36872 | tf_op jit(solution)/shard_map/ppermute | solution.py:29
  12.3 4.9 %collective-permute-start.2 = (bf16[6,1,1024]{2,1,0:T(2,128)(2,1)S(1)}, bf16[6,1,1024]{2,1,0:T(2,128)(2,1)S(1)}, u32[]{:S(2)}, u32[]{:S(2)}) collective-permute-start(bf16[6,1,1024]{2,1,0:T(2,128)(2,1)S(1)} %get-tuple-element.29), channel_id=1, source_target_pairs={{0,1},{1,2},{2,3},{4,5},{5,6},{6,7},{8,9},{9,10},{10,11},{12,13},{... | collective-permute-start | bytes 36872 | tf_op jit(solution)/shard_map/ppermute | solution.py:27
  61.6 23.4 %all-to-all-start = ((bf16[64,4,1,256]{3,1,2,0:T(4,128)(2,1)}), bf16[64,4,1,256]{3,1,2,0:T(4,128)(2,1)S(1)}, u32[]{:S(2)}, u32[]{:S(2)}) async-start(bf16[64,4,1,256]{3,1,2,0:T(4,128)(2,1)} %constant_dynamic-update-slice_fusion.3), calls=%async_computation | async-start | bytes 262144 | tf_op jit(solution)/shard_map/all_to_all | solution.py:15
  74.7 0.7 copy-start.3
